TPU v7x, 128 devices: a whole 4x4x4 slice. The times are simulated.
128 devices in a mesh: cell: 8 (over z_lo, x), gene: 16 (over z_hi, y, core).
Axes of the slice: x: 4, y: 4, z: 4 (z_hi: 2, z_lo: 2; z = z_hi * 2 + z_lo), core: 2. Of those that a mesh axis runs over, the one named last changes fastest.
Arguments:
- expression: bfloat16 [8192, 30720], P('cell', 'gene'), may hold values from -12 to 12
- prior_values: bfloat16 [30720, 1792], P('gene'), may hold values from -0.0625 to 0.0625
- block_mask: int32 [240, 14], P('gene'), may hold values 0 or 1
- gram_inverse: bfloat16 [1792, 1792], P(None, 'gene'), may hold values from -1 to 2
Outputs:
- coefficients: float32 [1792, 30720], P('cell', 'gene')
All inputs are finite; a program needn't handle non-finite values. No bound on the sum of `block_mask` on one device may be relied on, other than what follows from the above.
Results may differ from a plain program's by a relative error of at most 0.025.
Values may be sent and summed in bfloat16 or wider, within the bound.
A program may use at most 128 MiB of HBM per device.

v0:
```python
import jax
import jax.numpy as jnp
from jax import lax
from jax.sharding import PartitionSpec as P

BLOCK = 128
ITERS = 2
OUT_UNITS = 100.0
LASSO = 0.006
RIDGE = 0.1
PRIOR_RELIEF = 0.7
EPSILON = 1e-06


def shrink(moved, limit, step_size):
    kept = jnp.maximum(moved - limit, 0.0) - jnp.maximum(-moved - limit, 0.0)
    return kept / (1.0 + step_size * RIDGE)


def on_device(expression, prior_values, block_mask, gram_inverse):
    cell_devices = lax.axis_size("cell")
    cell_rows, gene_rows = expression.shape
    tf_total = prior_values.shape[1]
    gene_blocks, tf_blocks = block_mask.shape
    support = block_mask.astype(jnp.bfloat16)[:, None, :, None]
    masked = (prior_values.reshape(gene_blocks, BLOCK, tf_blocks, BLOCK) * support).reshape(
        gene_rows, tf_total
    )
    tf_scores = lax.psum_scatter(
        lax.dot_general(
            masked, expression, (((0,), (1,)), ((), ())), preferred_element_type=jnp.float32
        ).astype(jnp.bfloat16),
        "gene",
        scatter_dimension=0,
        tiled=True,
    )
    activity_part = lax.dot_general(
        gram_inverse,
        lax.all_gather(tf_scores, "gene", axis=0, tiled=True),
        (((0,), (0,)), ((), ())),
        preferred_element_type=jnp.float32,
    ).astype(jnp.bfloat16)
    activity_t = lax.all_gather(activity_part, "gene", axis=0, tiled=True)
    widened = activity_t.astype(jnp.float32)
    sum_squares = lax.psum(jnp.sum(widened * widened), "cell")
    total_cells = cell_rows * cell_devices
    step_size = 0.5 / (sum_squares / (total_cells * tf_total) + EPSILON)
    relief = block_mask.T.astype(jnp.float32)[:, None, :, None]
    penalty = jnp.broadcast_to(1.0 - PRIOR_RELIEF * relief, (tf_blocks, BLOCK, gene_blocks, BLOCK))
    limit = step_size * LASSO * penalty.reshape(tf_total, gene_rows)
    tf_rows = tf_total // cell_devices
    first_row = lax.axis_index("cell") * tf_rows
    coefficient_bf = jnp.zeros((tf_total, gene_rows), jnp.bfloat16)
    coefficient = jnp.zeros((tf_total, gene_rows), jnp.float32)
    for sweep in range(ITERS):
        if sweep == 0:
            residual = -expression
        else:
            fitted = lax.dot_general(
                activity_t,
                coefficient_bf,
                (((0,), (0,)), ((), ())),
                preferred_element_type=jnp.float32,
            )
            residual = (fitted - expression.astype(jnp.float32)).astype(jnp.bfloat16)
        partial_term = jnp.dot(activity_t, residual, preferred_element_type=jnp.float32)
        gradient = (
            lax.psum(partial_term.astype(jnp.bfloat16), "cell").astype(jnp.float32) / total_cells
        )
        coefficient = shrink(coefficient - step_size * gradient, limit, step_size)
        coefficient_bf = coefficient.astype(jnp.bfloat16)
    coefficient = lax.dynamic_slice_in_dim(coefficient, first_row, tf_rows, 0)
    return coefficient * OUT_UNITS


def solution(mesh):
    in_specs = (P("cell", "gene"), P("gene", None), P("gene", None), P(None, "gene"))
    out_specs = P("cell", "gene")
    return jax.shard_map(
        on_device, mesh=mesh, in_specs=in_specs, out_specs=out_specs, check_vma=False
    )
```

profile of v0, /device:TPU:1, one launch (start us, length us, event | category | flops | bytes accessed | tf_op | source)
XLA Modules:
  0.0 598.1 jit_solution(4196749134953552201)
XLA Ops:
  6.5 0.0 copy-start
  6.5 0.0 reduce-scatter.2.cloned.1.call-start
  6.5 0.8 convert_element_type.40
  7.3 0.1 copy.6
  7.4 9.8 %copy.7 = bf16[1920,1792]{0,1:T(8,128)(2,1)} copy(bf16[1920,1792]{1,0:T(8,128)(2,1)} %param.5) | data formatting | bytes 13762560 | tf_op args[1]
  17.2 0.0 copy-start.3
  17.2 1.0 mul.63
  18.3 1.9 copy-done.3
  20.2 11.3 %fusion.5 = bf16[1792,1024]{1,0:T(8,128)(2,1)} fusion(bf16[1024,1920]{1,0:T(8,128)(2,1)} %param.4, bf16[1920,1792]{0,1:T(8,128)(2,1)S(1)} %copy-done.3, bf16[224,8,15,128]{3,2,1,0:T(8,128)(2,1)S(1)} %bitcast.25), kind=kOutput, calls=%fused_computation.13 | convolution fusion | flops 7051706368 | bytes 21364736 | tf_op jit(solution)/shard_map/dot_general | solution.py:30
  31.5 0.0 reduce-scatter.2.cloned.1.call-update
  31.5 0.0 all-gather.3.cloned.1.call-start
  31.6 79.6 %reduce-scatter.2.cloned.1.call-done = bf16[112,1024]{1,0:T(8,128)(2,1)} async-done(((bf16[1792,1024]{1,0:T(8,128)(2,1)}), bf16[112,1024]{1,0:T(8,128)(2,1)}) %reduce-scatter.2.cloned.1.call-update) | async-done | bytes 229392 | tf_op jit(solution)/shard_map/reduce_scatter | solution.py:29
  111.2 0.0 all-gather.3.cloned.1.call-update
  111.2 0.0 all-gather.5.cloned.1.call-start
  111.2 56.9 %all-gather.3.cloned.1.call-done = bf16[1792,1024]{1,0:T(8,128)(2,1)} async-done(((bf16[112,1024]{1,0:T(8,128)(2,1)}), bf16[1792,1024]{1,0:T(8,128)(2,1)}) %all-gather.3.cloned.1.call-update) | async-done | bytes 3670032 | tf_op jit(solution)/shard_map/all_gather | solution.py:39
  168.1 0.0 copy-done
  168.1 3.4 fusion.6
  171.5 0.0 all-gather.5.cloned.1.call-update
  171.5 0.0 all-reduce.3.cloned.1.call-start
  171.6 52.9 %all-gather.5.cloned.1.call-done = bf16[1792,1024]{1,0:T(8,128)(2,1)} async-done(((bf16[112,1024]{1,0:T(8,128)(2,1)}), bf16[1792,1024]{1,0:T(8,128)(2,1)}) %all-gather.5.cloned.1.call-update) | async-done | bytes 3670032 | tf_op jit(solution)/shard_map/all_gather | solution.py:43
  224.5 12.5 %convolution_convert_fusion.1 = bf16[1792,1920]{1,0:T(8,128)(2,1)} fusion(bf16[1792,1024]{1,0:T(8,128)(2,1)} %all-gather.5.cloned.1.call-done, bf16[1024,1920]{1,0:T(8,128)(2,1)} %param.4), kind=kOutput, calls=%fused_computation.5 | convolution fusion | flops 7051837440 | bytes 14483456 | tf_op jit(solution)/shard_map/dot_general | solution.py:66
  236.9 0.0 copy-start.5
  236.9 0.0 all-reduce.3.cloned.1.call-update
  237.0 0.0 all-reduce.5.cloned.1.call-start
  237.0 4.5 multiply_reduce_fusion
  241.6 18.2 %psum.22 = f32[]{:T(128)} all-reduce(f32[]{:T(128)} %multiply_reduce_fusion), channel_id=1, replica_groups=mesh['cell'=8,'gene'=16] {'cell'}, use_global_device_ids=true, to_apply=%region_3.0 | all-reduce | flops 1 | bytes 8 | tf_op jit(solution)/shard_map/psum | solution.py:45
  260.5 0.0 copy-done.5
  260.5 0.1 copy.8
  260.6 130.6 %all-reduce.3.cloned.1.call-done = bf16[1792,1920]{1,0:T(8,128)(2,1)} async-done(((bf16[1792,1920]{1,0:T(8,128)(2,1)}), bf16[1792,1920]{1,0:T(8,128)(2,1)}) %all-reduce.3.cloned.1.call-update) | async-done | bytes 6881296 | tf_op jit(solution)/shard_map/psum | solution.py:68
  391.2 0.0 copy-start.2
  391.2 1.0 broadcast_in_dim.2
  392.2 1.9 copy-done.2
  394.1 0.0 copy-start.4
  394.1 13.1 %subtract_divide_fusion = (f32[1792,1920]{1,0:T(8,128)}, f32[1792,1920]{1,0:T(8,128)}) fusion(bf16[1792,1920]{1,0:T(8,128)(2,1)S(1)} %copy-done.2, f32[]{:T(128)S(6)} %add.19, f32[]{:T(128)S(6)} %mul.67, f32[224,8,15,128]{3,2,1,0:T(8,128)S(1)} %bitcast.24), kind=kLoop, calls=%fused_computation.2 | loop fusion | flops 34406400 | bytes 48168968 | tf_op jit(solution)/shard_map/div | solution.py:17
  407.2 0.0 copy-done.4
  407.2 0.0 copy-start.6
  407.2 11.8 %fusion.2 = f32[1024,1920]{1,0:T(8,128)S(1)} fusion(bf16[1792,1024]{1,0:T(8,128)(2,1)S(1)} %copy-done.4, f32[1792,1920]{1,0:T(8,128)} %get-tuple-element.5), kind=kOutput, calls=%fused_computation.10 | convolution fusion | flops 7049871360 | bytes 25296896 | tf_op jit(solution)/shard_map/dot_general | solution.py:59
  419.0 0.0 copy-done.6
  419.0 9.9 %convolution_convert_fusion = bf16[1792,1920]{1,0:T(8,128)(2,1)} fusion(bf16[1792,1024]{1,0:T(8,128)(2,1)S(1)} %copy-done.4, f32[1024,1920]{1,0:T(8,128)S(1)} %fusion.2, bf16[1024,1920]{1,0:T(8,128)(2,1)S(1)} %copy-done.6), kind=kOutput, calls=%fused_computation.4 | convolution fusion | flops 7055769600 | bytes 22347776 | tf_op jit(solution)/shard_map/dot_general | solution.py:66
  428.9 0.0 all-reduce.5.cloned.1.call-update
  428.9 154.9 %all-reduce.5.cloned.1.call-done = bf16[1792,1920]{1,0:T(8,128)(2,1)} async-done(((bf16[1792,1920]{1,0:T(8,128)(2,1)}), bf16[1792,1920]{1,0:T(8,128)(2,1)}) %all-reduce.5.cloned.1.call-update) | async-done | bytes 6881296 | tf_op jit(solution)/shard_map/psum | solution.py:68
  583.9 0.0 copy-start.1
  583.9 3.9 convert_multiply_fusion
  587.8 3.8 divide_multiply_fusion
  591.5 0.0 copy-done.1
  (1 shorter events, 0.0 us)
Async XLA Ops:
  6.5 161.6 %copy-start = (bf16[1792,112]{0,1:T(8,128)(2,1)S(1)}, bf16[1792,112]{0,1:T(8,128)(2,1)}, u32[]{:S(2)}) copy-start(bf16[1792,112]{0,1:T(8,128)(2,1)} %param.7) | copy-start | bytes 1204228
  6.5 104.6 %reduce-scatter.2.cloned.1.call-start = ((), (), s32[]{:S(2)}) async-start(), calls=%async_computation.1 | async-start | bytes 3899392 | tf_op jit(solution)/shard_map/reduce_scatter | solution.py:29
  17.2 3.0 copy-start.3
  31.5 136.6 %all-gather.3.cloned.1.call-start = ((), (), s32[]{:S(2)}) async-start(), calls=%async_computation.2 | async-start | bytes 3899392 | tf_op jit(solution)/shard_map/all_gather | solution.py:39
  111.2 113.3 %all-gather.5.cloned.1.call-start = ((), (), s32[]{:S(2)}) async-start(), calls=%async_computation.3 | async-start | bytes 3899392 | tf_op jit(solution)/shard_map/all_gather | solution.py:43
  171.5 219.6 %all-reduce.3.cloned.1.call-start = ((), (), s32[]{:S(2)}) async-start(), calls=%async_computation.4 | async-start | bytes 13762560 | tf_op jit(solution)/shard_map/psum | solution.py:68
  236.9 23.5 %copy-start.5 = (s32[15,14]{1,0:T(8,128)S(1)}, s32[15,14]{1,0:T(8,128)}, u32[]{:S(2)}) copy-start(s32[15,14]{1,0:T(8,128)} %param.6) | copy-start | bytes 2524
  237.0 346.9 %all-reduce.5.cloned.1.call-start = ((), (), s32[]{:S(2)}) async-start(), calls=%async_computation.5 | async-start | bytes 13762560 | tf_op jit(solution)/shard_map/psum | solution.py:68
  391.2 3.0 copy-start.2
  394.1 13.1 %copy-start.4 = (bf16[1792,1024]{1,0:T(8,128)(2,1)S(1)}, bf16[1792,1024]{1,0:T(8,128)(2,1)}, u32[]{:S(2)}) copy-start(bf16[1792,1024]{1,0:T(8,128)(2,1)} %all-gather.5.cloned.1.call-done) | copy-start | bytes 11010052
  407.2 11.8 %copy-start.6 = (bf16[1024,1920]{1,0:T(8,128)(2,1)S(1)}, bf16[1024,1920]{1,0:T(8,128)(2,1)}, u32[]{:S(2)}) copy-start(bf16[1024,1920]{1,0:T(8,128)(2,1)} %param.4) | copy-start | bytes 11796484
  583.9 7.7 %copy-start.1 = (bf16[1792,112]{0,1:T(8,128)(2,1)S(1)}, bf16[1792,112]{0,1:T(8,128)(2,1)}, u32[]{:S(2)}) copy-start(bf16[1792,112]{0,1:T(8,128)(2,1)} %param.7) | copy-start | bytes 1204228
Sparse Core Ops, SparseCore 0:
  31.7 79.4 reduce-scatter.1
  113.6 54.4 all-gather.2
  171.7 52.7 all-gather.4
  237.1 154.0 all-reduce.2
  429.1 154.7 all-reduce.4
where the time goes:
time: 599 us; the launch traced here: 598 us
  waiting for transfers between devices  475 us (79%)
  matrix products  48.9 us (8%)
  other arithmetic  26 us (4%)
  blocking collectives  18.2 us (3%)
  local copies, waits for them, and re-layouts  15.9 us (3%)
  between operations  13.9 us (2%)
    psum x2, waiting for transfers between devices, on_device(): lax.psum(partial_term.astype(jnp.bfloat16), 'cell').astype(jnp.float32)  286 us
    reduce_scatter x1, waiting for transfers between devices, on_device(): lax.psum_scatter(lax.dot_general(masked, expression, (((0,), (1,)), ((),...  79.6 us
    all_gather x1, waiting for transfers between devices, on_device(): lax.all_gather(tf_scores, 'gene', axis=0, tiled=True)  56.9 us
    all_gather x1, waiting for transfers between devices, on_device(): activity_t = lax.all_gather(activity_part, 'gene', axis=0, tiled=True)  52.9 us
    dot_general x2, matrix products, on_device(): jnp.dot(activity_t, residual, preferred_element_type=jnp.float32)  22.4 us
    psum x1, blocking collectives, on_device(): sum_squares = lax.psum(jnp.sum(widened * widened), 'cell')  18.2 us
    unnamed x15, local copies, waits for them, and re-layouts  13.7 us
    div x1, other arithmetic, shrink(): return kept / (1.0 + step_size * RIDGE)  13.1 us
  transfers between devices with their start and end apart: 5, of which 5 were waited for; matrix products, arithmetic and copies ran while one was open for 1% of the time, Pallas kernels for 0%

commit v1 on v0

--- a/solution.py
+++ b/solution.py
@@ -65,7 +65,10 @@
             residual = (fitted - expression.astype(jnp.float32)).astype(jnp.bfloat16)
         partial_term = jnp.dot(activity_t, residual, preferred_element_type=jnp.float32)
         gradient = (
-            lax.psum(partial_term.astype(jnp.bfloat16), "cell").astype(jnp.float32) / total_cells
+            jnp.sum(lax.all_gather(partial_term.astype(jnp.bfloat16), "cell"), axis=0).astype(
+                jnp.float32
+            )
+            / total_cells
         )
         coefficient = shrink(coefficient - step_size * gradient, limit, step_size)
         coefficient_bf = coefficient.astype(jnp.bfloat16)

time: 599 us -> 1390 us (2.32)
  waiting for transfers between devices: 475 us -> 1220 us
  other arithmetic: 26 us -> 71.1 us
    all_gather x0 -> x2, waiting for transfers between devices: none -> 1030 us  [on_device(): lax.all_gather(partial_term.astype(jnp.bfloat16), 'cell')]
    psum x2 -> x0, waiting for transfers between devices: 286 us -> none  [on_device(): lax.psum(partial_term.astype(jnp.bfloat16), 'cell').astype(jnp.float32)]
    reduce_sum x0 -> x2, other arithmetic: none -> 45.1 us  [on_device(): jnp.sum(lax.all_gather(partial_term.astype(jnp.bfloat16), 'cell'), axis=0)]
  transfers between devices with their start and end apart: 5 -> 5, of which waited for: 5 -> 5; matrix products, arithmetic and copies ran while one was open for 1% -> 0% of each run, Pallas kernels for 0% -> 0%
where the time goes in v1:
time: 1390 us
  waiting for transfers between devices  1220 us (88%)
  other arithmetic  71.1 us (5%)
  matrix products  49.1 us (4%)
  blocking collectives  18.2 us (1%)
  local copies, waits for them, and re-layouts  15.9 us (1%)
  between operations  13.9 us (1%)
    all_gather x2, waiting for transfers between devices, on_device(): lax.all_gather(partial_term.astype(jnp.bfloat16), 'cell')  1030 us
    reduce_scatter x1, waiting for transfers between devices, on_device(): lax.psum_scatter(lax.dot_general(masked, expression, (((0,), (1,)), ((),...  79.6 us
    all_gather x1, waiting for transfers between devices, on_device(): lax.all_gather(tf_scores, 'gene', axis=0, tiled=True)  56.9 us
    all_gather x1, waiting for transfers between devices, on_device(): activity_t = lax.all_gather(activity_part, 'gene', axis=0, tiled=True)  52.9 us
    reduce_sum x2, other arithmetic, on_device(): jnp.sum(lax.all_gather(partial_term.astype(jnp.bfloat16), 'cell'), axis=0)  45.1 us
  transfers between devices with their start and end apart: 5, of which 5 were waited for; matrix products, arithmetic and copies ran while one was open for 0% of the time, Pallas kernels for 0%

profile of v1, /device:TPU:1, one launch (start us, length us, event | category | flops | bytes accessed | tf_op | source)
XLA Modules:
  0.0 1390.1 jit_solution(14973730892128118926)
XLA Ops:
  6.5 0.0 copy-start
  6.5 0.0 reduce-scatter.2.cloned.1.call-start
  6.5 0.8 convert_element_type.44
  7.3 0.1 copy.6
  7.4 9.8 copy.7
  17.2 0.0 copy-start.3
  17.2 1.0 mul.63
  18.3 1.9 copy-done.3
  20.2 11.3 fusion.5
  31.5 0.0 reduce-scatter.2.cloned.1.call-update
  31.5 0.0 all-gather.7.cloned.1.call-start
  31.6 79.6 %reduce-scatter.2.cloned.1.call-done = bf16[112,1024]{1,0:T(8,128)(2,1)} async-done(((bf16[1792,1024]{1,0:T(8,128)(2,1)}), bf16[112,1024]{1,0:T(8,128)(2,1)}) %reduce-scatter.2.cloned.1.call-update) | async-done | bytes 229392 | tf_op jit(solution)/shard_map/reduce_scatter | solution.py:29
  111.2 0.0 all-gather.7.cloned.1.call-update
  111.2 0.0 all-gather.9.cloned.1.call-start
  111.2 56.9 %all-gather.7.cloned.1.call-done = bf16[1792,1024]{1,0:T(8,128)(2,1)} async-done(((bf16[112,1024]{1,0:T(8,128)(2,1)}), bf16[1792,1024]{1,0:T(8,128)(2,1)}) %all-gather.7.cloned.1.call-update) | async-done | bytes 3670032 | tf_op jit(solution)/shard_map/all_gather | solution.py:39
  168.1 0.0 copy-done
  168.1 3.4 fusion.6
  171.5 0.0 all-gather.9.cloned.1.call-update
  171.5 0.0 all-gather.11.cloned.1.call-start
  171.6 52.9 %all-gather.9.cloned.1.call-done = bf16[1792,1024]{1,0:T(8,128)(2,1)} async-done(((bf16[112,1024]{1,0:T(8,128)(2,1)}), bf16[1792,1024]{1,0:T(8,128)(2,1)}) %all-gather.9.cloned.1.call-update) | async-done | bytes 3670032 | tf_op jit(solution)/shard_map/all_gather | solution.py:43
  224.5 12.3 convolution_convert_fusion.1
  236.8 0.0 copy-start.5
  236.8 0.0 all-gather.11.cloned.1.call-update
  236.8 0.0 all-gather.13.cloned.1.call-start
  236.9 4.5 multiply_reduce_fusion
  241.4 18.2 %psum.7 = f32[]{:T(128)} all-reduce(f32[]{:T(128)} %multiply_reduce_fusion), channel_id=1, replica_groups=mesh['cell'=8,'gene'=16] {'cell'}, use_global_device_ids=true, to_apply=%region_3.0 | all-reduce | flops 1 | bytes 8 | tf_op jit(solution)/shard_map/psum | solution.py:45
  260.3 0.0 copy-done.5
  260.3 0.1 copy.8
  260.4 504.2 %all-gather.11.cloned.1.call-done = bf16[14336,1920]{1,0:T(8,128)(2,1)} async-done(((bf16[1792,1920]{1,0:T(8,128)(2,1)}), bf16[14336,1920]{1,0:T(8,128)(2,1)}) %all-gather.11.cloned.1.call-update) | async-done | bytes 55050256 | tf_op jit(solution)/shard_map/all_gather | solution.py:68
  764.7 22.5 %reduce_sum.33 = bf16[1792,1920]{1,0:T(8,128)(2,1)} reduce(bf16[8,1792,1920]{2,1,0:T(8,128)(2,1)} %bitcast.27, bf16[]{:T(256)} %constant.7.clone.1), dimensions={0}, to_apply=%region_1.0 | reduce | flops 24084480 | bytes 61931520 | tf_op jit(solution)/shard_map/reduce_sum | solution.py:68
  787.2 0.0 copy-start.2
  787.2 1.0 broadcast_in_dim.2
  788.2 1.9 copy-done.2
  790.1 0.0 copy-start.4
  790.1 13.1 subtract_divide_fusion
  803.2 0.0 copy-done.4
  803.2 0.0 copy-start.6
  803.2 11.8 fusion.2
  815.0 0.0 copy-done.6
  815.0 10.2 convolution_convert_fusion
  825.3 0.0 all-gather.13.cloned.1.call-update
  825.3 528.1 %all-gather.13.cloned.1.call-done = bf16[14336,1920]{1,0:T(8,128)(2,1)} async-done(((bf16[1792,1920]{1,0:T(8,128)(2,1)}), bf16[14336,1920]{1,0:T(8,128)(2,1)}) %all-gather.13.cloned.1.call-update) | async-done | bytes 55050256 | tf_op jit(solution)/shard_map/all_gather | solution.py:68
  1353.4 22.6 %reduce_sum.35 = bf16[1792,1920]{1,0:T(8,128)(2,1)} reduce(bf16[8,1792,1920]{2,1,0:T(8,128)(2,1)} %bitcast.28, bf16[]{:T(256)} %constant.7.clone.1), dimensions={0}, to_apply=%region_4.0 | reduce | flops 24084480 | bytes 61931520 | tf_op jit(solution)/shard_map/reduce_sum | solution.py:68
  1375.9 0.0 copy-start.1
  1375.9 3.9 convert_multiply_fusion
  1379.8 3.8 divide_multiply_fusion
  1383.6 0.0 copy-done.1
  (1 shorter events, 0.0 us)
Async XLA Ops:
  6.5 161.6 %copy-start = (bf16[1792,112]{0,1:T(8,128)(2,1)S(1)}, bf16[1792,112]{0,1:T(8,128)(2,1)}, u32[]{:S(2)}) copy-start(bf16[1792,112]{0,1:T(8,128)(2,1)} %param.7) | copy-start | bytes 1204228
  6.5 104.6 %reduce-scatter.2.cloned.1.call-start = ((), (), s32[]{:S(2)}) async-start(), calls=%async_computation.1 | async-start | bytes 3899392 | tf_op jit(solution)/shard_map/reduce_scatter | solution.py:29
  17.2 3.0 copy-start.3
  31.5 136.6 %all-gather.7.cloned.1.call-start = ((), (), s32[]{:S(2)}) async-start(), calls=%async_computation.2 | async-start | bytes 3899392 | tf_op jit(solution)/shard_map/all_gather | solution.py:39
  111.2 113.3 %all-gather.9.cloned.1.call-start = ((), (), s32[]{:S(2)}) async-start(), calls=%async_computation.3 | async-start | bytes 3899392 | tf_op jit(solution)/shard_map/all_gather | solution.py:43
  171.5 593.1 %all-gather.11.cloned.1.call-start = ((), (), s32[]{:S(2)}) async-start(), calls=%async_computation.4 | async-start | bytes 61931520 | tf_op jit(solution)/shard_map/all_gather | solution.py:68
  236.8 23.5 %copy-start.5 = (s32[15,14]{1,0:T(8,128)S(1)}, s32[15,14]{1,0:T(8,128)}, u32[]{:S(2)}) copy-start(s32[15,14]{1,0:T(8,128)} %param.6) | copy-start | bytes 2524
  236.8 1116.5 %all-gather.13.cloned.1.call-start = ((), (), s32[]{:S(2)}) async-start(), calls=%async_computation.5 | async-start | bytes 61931520 | tf_op jit(solution)/shard_map/all_gather | solution.py:68
  787.2 3.0 copy-start.2
  790.1 13.1 copy-start.4
  803.2 11.8 copy-start.6
  1375.9 7.7 copy-start.1
Sparse Core Ops, SparseCore 0:
  31.7 79.4 reduce-scatter.1
  113.6 54.4 all-gather.6
  171.7 52.7 all-gather.8
  236.9 527.6 all-gather.10
  825.4 527.9 all-gather.12
